TPU v7x, 32 devices: a whole 2x2x4 slice. The times are simulated.
32 devices in a mesh: seq: 4 (over y, x), img: 2 (over core), dp: 4 (over z).
Axes of the slice: x: 2, y: 2, z: 4, core: 2. Of those that a mesh axis runs over, the one named last changes fastest.
Arguments:
- queries: bfloat16 [512, 8192], P('seq', 'dp'), may hold values from -22 to 22
- out_grad: bfloat16 [512, 8192], P('seq', 'dp'), may hold values from -600 to 600
- token_image: int32 [512], P('seq'), may hold values from -1 to 1, as said below
- unnormed_keys: bfloat16 [2, 6432, 1024], P('img', 'seq', 'dp'), may hold values from -14 to 14
- values: bfloat16 [2, 6432, 1024], P('img', 'seq', 'dp'), may hold values from -6 to 6
- key_gain: float32 [128], replicated, may hold values from 0.1 to 1.9
- tile_count: int32 [2], replicated, may hold values from 1 to 4, as said below
- key_projection_matrix: bfloat16 [8192, 1024], P('dp', 'seq'), may hold values from -0.1875 to 0.1875
- value_projection_matrix: bfloat16 [8192, 1024], P('dp', 'seq'), may hold values from -0.1875 to 0.1875
Outputs:
- feature_grad: bfloat16 [2, 6432, 8192], P('img', 'seq', 'dp')
Inputs may be any that keep to these rules, and one draw needn't show every extreme that they name: `token_image`: in each block of 128 tokens (one index of seq) at most 16 tokens name one image, and some image is named by exactly 16; -1 marks a token that attends no image. `tile_count`: some image has 4 tiles.
All inputs are finite; a program needn't handle non-finite values.
Results may differ from a plain program's by a relative error of at most 0.0067.
Values may be sent and summed in bfloat16 or wider, within the bound.
A program may use at most 128 MiB of HBM per device.

v0:
```python
import functools

import jax
import jax.numpy as jnp
from jax import lax
from jax.experimental import pallas as pl
from jax.experimental.pallas import tpu as pltpu
from jax.sharding import PartitionSpec as P

QUERY_HEAD_COUNT = 64
KEY_VALUE_HEADS = 8
HEAD_WIDTH = 128
TILE_TOK = 1601
TILE_ROWS = 1608
CAP = 16


epsilon = 1e-05
masked = -1e30


def body_any(
    queries,
    out_grad,
    token_image,
    unnormed_keys,
    values,
    key_gain,
    tile_count,
    key_projection_matrix,
    value_projection_matrix,
):
    image_number = lax.axis_index("img")
    seq_index = lax.axis_index("seq")
    attends = token_image == image_number
    slot_rank = jnp.cumsum(attends.astype(jnp.int32)) - 1
    picker = (
        attends[None, :] & (slot_rank[None, :] == jnp.arange(CAP, dtype=jnp.int32)[:, None])
    ).astype(jnp.bfloat16)
    packed_query = jnp.dot(picker, queries, preferred_element_type=jnp.float32).astype(jnp.bfloat16)
    packed_grad = jnp.dot(picker, out_grad, preferred_element_type=jnp.float32).astype(jnp.bfloat16)
    text_query, text_grad = (
        lax.all_gather(packed_query, "seq", axis=0, tiled=True),
        lax.all_gather(packed_grad, "seq", axis=0, tiled=True),
    )
    key_rows = unnormed_keys.shape[1]
    key_width = unnormed_keys.shape[2]
    key_heads = key_width // HEAD_WIDTH
    group_length = QUERY_HEAD_COUNT // KEY_VALUE_HEADS
    text_rows = text_query.shape[0]
    score_scale = HEAD_WIDTH ** (-0.5)
    unnormed_float = unnormed_keys[0].astype(jnp.float32).reshape(key_rows, key_heads, HEAD_WIDTH)
    inverse = lax.rsqrt(jnp.mean(unnormed_float * unnormed_float, axis=-1, keepdims=True) + epsilon)
    unit_key = unnormed_float * inverse
    normed = (unit_key * key_gain).astype(jnp.bfloat16)
    value_heads = values[0].reshape(key_rows, key_heads, HEAD_WIDTH)
    query_heads = text_query.reshape(text_rows, key_heads, group_length, HEAD_WIDTH)
    grad_heads = text_grad.reshape(text_rows, key_heads, group_length, HEAD_WIDTH)
    row_global = seq_index * key_rows + jnp.arange(key_rows, dtype=jnp.int32)
    tile_limit = jnp.sum(
        jnp.where(jnp.arange(tile_count.shape[0], dtype=jnp.int32) == image_number, tile_count, 0)
    )
    live_rows = (row_global // TILE_ROWS < tile_limit) & (row_global % TILE_ROWS < TILE_TOK)
    scores = (
        jnp.einsum("rhge,khe->hgrk", query_heads, normed, preferred_element_type=jnp.float32)
        * score_scale
    )
    scores = jnp.where(live_rows, scores, masked)
    grad_probs = jnp.einsum(
        "rhge,khe->hgrk", grad_heads, value_heads, preferred_element_type=jnp.float32
    )
    row_top = lax.pmax(jnp.max(scores, axis=-1), "seq")
    exponent = jnp.exp(scores - row_top[..., None])
    row_total = lax.psum(jnp.sum(exponent, axis=-1), "seq")
    probabilities = exponent / row_total[..., None]
    inner_sum = lax.psum(jnp.sum(probabilities * grad_probs, axis=-1), "seq")
    probs_low = probabilities.astype(jnp.bfloat16)
    score_grad = (probabilities * (grad_probs - inner_sum[..., None])).astype(jnp.bfloat16)
    value_gradient = jnp.einsum(
        "hgrk,rhge->khe", probs_low, grad_heads, preferred_element_type=jnp.float32
    )
    normalized_gradient = (
        jnp.einsum("hgrk,rhge->khe", score_grad, query_heads, preferred_element_type=jnp.float32)
        * score_scale
    )
    unit_grad = normalized_gradient * key_gain
    key_gradient = inverse * (
        unit_grad - unit_key * jnp.mean(unit_grad * unit_key, axis=-1, keepdims=True)
    )
    key_reduced_precision = key_gradient.astype(jnp.bfloat16).reshape(key_rows, key_width)
    value_reduced_precision = value_gradient.astype(jnp.bfloat16).reshape(key_rows, key_width)
    key_all, value_all = (
        lax.all_gather(key_reduced_precision, "dp", axis=1, tiled=True),
        lax.all_gather(value_reduced_precision, "dp", axis=1, tiled=True),
    )
    contracting = (((1,), (1,)), ((), ()))
    partial_value = lax.dot_general(
        key_all,
        lax.all_gather(key_projection_matrix, "seq", axis=1, tiled=True),
        contracting,
        preferred_element_type=jnp.float32,
    )
    feature_sum = partial_value + lax.dot_general(
        value_all,
        lax.all_gather(value_projection_matrix, "seq", axis=1, tiled=True),
        contracting,
        preferred_element_type=jnp.float32,
    )
    return feature_sum.astype(jnp.bfloat16)[None]


MESH = pl.DeviceIdType.MESH
NT = (((1,), (1,)), ((), ()))
NN = (((1,), (0,)), ((), ()))
CHUNK = 272
FEATURE_TILE = 256
VMEM_BYTES = 67043328


def dot(a, b, dims):
    return lax.dot_general(a, b, dims, preferred_element_type=jnp.float32)


def kernel(
    sizes,
    image_ref,
    limit_ref,
    query_hbm,
    grad_hbm,
    key_hbm,
    value_hbm,
    gain_ref,
    key_weight_ref,
    value_weight_ref,
    out_ref,
    query_ref,
    grad_ref,
    key_ref,
    value_ref,
    normed_ref,
    partial,
    text,
    score,
    grad_prob,
    stats,
    rows_all,
    weights,
    load_sem,
    text_send,
    text_recv,
    stat_send,
    stat_recv,
    weight_local,
    weight_send,
    weight_recv,
    relay_send,
    relay_recv,
    row_send,
    row_recv,
):
    n_seq, n_dp, heads, group = sizes
    seq = lax.axis_index("seq")
    img = lax.axis_index("img")
    dp = lax.axis_index("dp")
    rows, width = key_ref.shape
    features = key_weight_ref.shape[0]
    half = features // 2
    stack = group * CAP
    query_rows = n_seq * stack
    full = rows // CHUNK
    rest = rows - full * CHUNK
    padded = rows_all.shape[1]
    chunks = [(c * CHUNK, CHUNK) for c in range(full)] + [(full * CHUNK, padded - full * CHUNK)]
    scale = HEAD_WIDTH ** (-0.5)
    near, far = seq % 2, seq // 2
    seq_peers = [far * 2 + 1 - near, (1 - far) * 2 + near, (1 - far) * 2 + 1 - near]

    loads = [
        pltpu.make_async_copy(source, target, load_sem.at[k])
        for k, (source, target) in enumerate(
            (
                (query_hbm, query_ref),
                (grad_hbm, grad_ref),
                (key_hbm, key_ref),
                (value_hbm, value_ref),
            )
        )
    ]
    for copy in loads:
        copy.start()

    own_weights = [
        pltpu.make_async_copy(
            ref, weights.at[seq, :, pl.ds(k * width, width)], weight_local.at[k]
        )
        for k, ref in enumerate((key_weight_ref, value_weight_ref))
    ]
    barrier = pltpu.get_barrier_semaphore()
    for peer in seq_peers:
        pl.semaphore_signal(barrier, inc=1, device_id={"seq": peer}, device_id_type=MESH)
    pl.semaphore_signal(barrier, inc=1, device_id={"img": 1 - img}, device_id_type=MESH)
    for j in range(1, n_dp):
        pl.semaphore_signal(
            barrier, inc=1, device_id={"dp": lax.rem(dp + j, n_dp)}, device_id_type=MESH
        )

    tokens = image_ref.shape[1]
    attends = image_ref[...] == img
    upper = (
        lax.broadcasted_iota(jnp.int32, (tokens, tokens), 0)
        <= lax.broadcasted_iota(jnp.int32, (tokens, tokens), 1)
    ).astype(jnp.bfloat16)
    counts = dot(
        jnp.broadcast_to(attends.astype(jnp.float32), (CAP, tokens)).astype(jnp.bfloat16), upper, NN
    )
    slot = lax.broadcasted_iota(jnp.int32, (CAP, tokens), 0).astype(jnp.float32) + 1.0
    picker = jnp.where(attends & (counts == slot), 1.0, 0.0).astype(jnp.bfloat16)
    for k, ref in enumerate((query_ref, grad_ref)):
        loads[k].wait()
        packed = dot(picker, ref[...], NN).astype(jnp.bfloat16)
        for h in range(heads):
            for g in range(group):
                column = (h * group + g) * HEAD_WIDTH
                text[seq, k, h, g * CAP : (g + 1) * CAP, :] = packed[:, column : column + HEAD_WIDTH]

    pl.semaphore_wait(barrier, n_seq - 1 + 1 + n_dp - 1)

    def text_copy(owner, peer, j):
        return pltpu.make_async_remote_copy(
            src_ref=text.at[owner],
            dst_ref=text.at[owner],
            send_sem=text_send.at[j],
            recv_sem=text_recv.at[owner],
            device_id={"seq": peer},
            device_id_type=MESH,
        )

    for j, peer in enumerate(seq_peers):
        text_copy(seq, peer, j).start()

    gain = gain_ref[...]
    live_limit = limit_ref[img]

    def unit_of(row0, size, h):
        k = key_ref[pl.ds(row0, size), h * HEAD_WIDTH : (h + 1) * HEAD_WIDTH].astype(jnp.float32)
        inverse = lax.rsqrt(jnp.mean(k * k, axis=-1, keepdims=True) + epsilon)
        return k * inverse, inverse

    def heads_of(k, h):
        return text[:, k, h].reshape(query_rows, HEAD_WIDTH)

    for copy in own_weights:
        copy.start()
    for copy in loads[2:]:
        copy.wait()

    def normalize(row0, size):
        for h in range(heads):
            unit, _ = unit_of(row0, size, h)
            normed_ref[pl.ds(row0, size), h * HEAD_WIDTH : (h + 1) * HEAD_WIDTH] = (
                unit * gain
            ).astype(jnp.bfloat16)

    def over_chunks(act, carry):
        carry = lax.fori_loop(
            0, full, lambda i, c: act(pl.multiple_of(i * CHUNK, 16), CHUNK, c), carry
        )
        return act(full * CHUNK, rest, carry)

    def normalize_chunk(row0, size, carry):
        normalize(row0, size)
        return carry

    over_chunks(normalize_chunk, 0)

    for j, owner in enumerate([seq] + seq_peers):
        if j:
            text_copy(owner, owner, j - 1).wait_recv()
        lanes = pl.ds(pl.multiple_of(owner * stack, stack), stack)

        def first_pass(row0, size, tops):
            new_tops = []
            row = seq * rows + row0 + lax.broadcasted_iota(jnp.int32, (size, 1), 0)
            live = (row // TILE_ROWS < live_limit) & (row % TILE_ROWS < TILE_TOK)
            for h in range(heads):
                normed = normed_ref[pl.ds(row0, size), h * HEAD_WIDTH : (h + 1) * HEAD_WIDTH]
                s = jnp.where(live, dot(normed, text[owner, 0, h], NT) * scale, masked)
                score[h, pl.ds(row0, size), lanes] = s
                new_tops.append(jnp.maximum(tops[h], jnp.max(s, axis=0, keepdims=True)))
            return tuple(new_tops)

        tops = over_chunks(
            first_pass, tuple(jnp.full((1, stack), masked, jnp.float32) for _ in range(heads))
        )

        def second_pass(row0, size, sums):
            new_sums = []
            for h in range(heads):
                e = jnp.exp(score[h, pl.ds(row0, size), lanes] - tops[h])
                v = value_ref[pl.ds(row0, size), h * HEAD_WIDTH : (h + 1) * HEAD_WIDTH]
                p = dot(v, text[owner, 1, h], NT)
                score[h, pl.ds(row0, size), lanes] = e
                grad_prob[h, pl.ds(row0, size), lanes] = p
                new_sums.append(sums[2 * h] + jnp.sum(e, axis=0, keepdims=True))
                new_sums.append(sums[2 * h + 1] + jnp.sum(e * p, axis=0, keepdims=True))
            return tuple(new_sums)

        sums = over_chunks(
            second_pass, tuple(jnp.zeros((1, stack), jnp.float32) for _ in range(2 * heads))
        )
        for h in range(heads):
            columns = pl.ds(pl.multiple_of(h * query_rows + owner * stack, stack), stack)
            stats[seq, 0:1, columns] = tops[h]
            stats[seq, 1:2, columns] = sums[2 * h]
            stats[seq, 2:3, columns] = sums[2 * h + 1]
    stats[seq, 3:8, :] = jnp.zeros((5, heads * query_rows), jnp.float32)

    def stat_copy(owner, peer, j):
        return pltpu.make_async_remote_copy(
            src_ref=stats.at[owner],
            dst_ref=stats.at[owner],
            send_sem=stat_send.at[j],
            recv_sem=stat_recv.at[owner],
            device_id={"seq": peer},
            device_id_type=MESH,
        )

    for j, peer in enumerate(seq_peers):
        stat_copy(seq, peer, j).start()
    for copy in own_weights:
        copy.wait()
    for j, peer in enumerate(seq_peers):
        stat_copy(peer, peer, j).wait_recv()

    def weight_copy(owner, peer, j):
        part = weights.at[owner, pl.ds(pl.multiple_of(img * half, half), half)]
        return pltpu.make_async_remote_copy(
            src_ref=part,
            dst_ref=part,
            send_sem=weight_send.at[j],
            recv_sem=weight_recv.at[owner],
            device_id={"seq": peer},
            device_id_type=MESH,
        )

    def relay_copy(owner, j, which):
        part = weights.at[owner, pl.ds(pl.multiple_of(which * half, half), half)]
        return pltpu.make_async_remote_copy(
            src_ref=part,
            dst_ref=part,
            send_sem=relay_send.at[j],
            recv_sem=relay_recv.at[owner],
            device_id={"img": 1 - img},
            device_id_type=MESH,
        )

    for j, peer in enumerate(seq_peers):
        weight_copy(seq, peer, j).start()

    all_tops = [stats[i, 0:1, :] for i in range(n_seq)]
    top = functools.reduce(jnp.maximum, all_tops)
    factors = [jnp.exp(t - top) for t in all_tops]
    total = sum(f * stats[i, 1:2, :] for i, f in enumerate(factors))
    inner_all = sum(f * stats[i, 2:3, :] for i, f in enumerate(factors)) / total
    own_factor_all = jnp.exp(stats[seq, 0:1, :] - top) / total

    def row_copy(owner, row0, size, c, side, distance):
        part = rows_all.at[owner, pl.ds(row0, size)]
        return pltpu.make_async_remote_copy(
            src_ref=part,
            dst_ref=part,
            send_sem=row_send.at[side, distance, c],
            recv_sem=row_recv.at[owner, c],
            device_id={"dp": dp + 1 if side == 0 else dp - 1},
            device_id_type=MESH,
        )

    def forward(row0, size, c, distance, act):
        for side in range(2):
            owner = dp - distance if side == 0 else dp + distance
            if side == 0:
                sends = (owner >= 0) & (dp < n_dp - 1)
            else:
                sends = (owner < n_dp) & (dp > 0)

            @pl.when(sends)
            def _():
                act(row_copy(owner, row0, size, c, side, distance))

    def arrive(row0, size, c, distance):
        for side in range(2):
            owner = dp - distance if side == 0 else dp + distance

            @pl.when((owner >= 0) & (owner < n_dp))
            def _():
                row_copy(owner, row0, size, c, side, 0).wait_recv()

    def third_pass(row0, size):
        for h in range(heads):
            columns = slice(h * query_rows, (h + 1) * query_rows)
            p = score[h, pl.ds(row0, size), :] * own_factor_all[:, columns]
            g = (p * (grad_prob[h, pl.ds(row0, size), :] - inner_all[:, columns])).astype(jnp.bfloat16)
            value_gradient = dot(p.astype(jnp.bfloat16), heads_of(1, h), NN)
            unit_grad = dot(g, heads_of(0, h), NN) * scale * gain
            unit, inverse = unit_of(row0, size, h)
            key_gradient = inverse * (
                unit_grad - unit * jnp.mean(unit_grad * unit, axis=-1, keepdims=True)
            )
            lane = h * HEAD_WIDTH
            rows_all[dp, pl.ds(row0, size), lane : lane + HEAD_WIDTH] = key_gradient.astype(
                jnp.bfloat16
            )
            lane = lane + width
            rows_all[dp, pl.ds(row0, size), lane : lane + HEAD_WIDTH] = value_gradient.astype(
                jnp.bfloat16
            )

    def start(copy):
        copy.start()

    def own_chunk(i, _):
        row0 = pl.multiple_of(i * CHUNK, 16)
        third_pass(row0, CHUNK)
        forward(row0, CHUNK, i, 0, start)
        return 0

    lax.fori_loop(0, full, own_chunk, 0)
    third_pass(full * CHUNK, rest)
    forward(chunks[-1][0], chunks[-1][1], full, 0, start)

    for c, (row0, size) in enumerate(chunks):
        arrive(row0, size, c, 1)
        forward(row0, size, c, 1, start)
    for j, peer in enumerate(seq_peers):
        weight_copy(peer, peer, j).wait_recv()
        relay_copy(peer, j, img).start()
    for c, (row0, size) in enumerate(chunks):
        arrive(row0, size, c, 2)
        forward(row0, size, c, 2, start)
    for j, peer in enumerate(seq_peers):
        relay_copy(peer, j, 1 - img).wait_recv()

    def multiply(row0, size):
        def tile(i, _):
            column = pl.multiple_of(i * FEATURE_TILE, FEATURE_TILE)
            total = functools.reduce(
                jnp.add,
                [
                    dot(
                        rows_all[b, pl.ds(row0, size), :],
                        weights[b, pl.ds(column, FEATURE_TILE), :],
                        NT,
                    )
                    for b in range(n_dp)
                ],
            )
            out_ref[pl.ds(row0, size), pl.ds(column, FEATURE_TILE)] = total.astype(out_ref.dtype)
            return 0

        lax.fori_loop(0, features // FEATURE_TILE, tile, 0)

    def finish_chunk(i, _):
        row0 = pl.multiple_of(i * CHUNK, 16)
        arrive(row0, CHUNK, i, 3)
        multiply(row0, CHUNK)
        return 0

    upper_half = dp // (n_dp // 2)
    farthest = (n_dp - 1) * (1 - upper_half)

    def last_product(block, column):
        return dot(
            rows_all[block, full * CHUNK : rows, :],
            weights[block, pl.ds(column, FEATURE_TILE), :],
            NT,
        )

    def partial_tile(i, _):
        column = pl.multiple_of(i * FEATURE_TILE, FEATURE_TILE)
        partial[:, pl.ds(column, FEATURE_TILE)] = functools.reduce(
            jnp.add, [last_product(upper_half + b, column) for b in range(n_dp - 1)]
        )
        return 0

    def last_tile(i, _):
        column = pl.multiple_of(i * FEATURE_TILE, FEATURE_TILE)
        total = partial[:, pl.ds(column, FEATURE_TILE)] + last_product(farthest, column)
        out_ref[full * CHUNK : rows, pl.ds(column, FEATURE_TILE)] = total.astype(out_ref.dtype)
        return 0

    lax.fori_loop(0, features // FEATURE_TILE, partial_tile, 0)
    lax.fori_loop(0, full, finish_chunk, 0)
    arrive(chunks[-1][0], chunks[-1][1], full, 3)
    lax.fori_loop(0, features // FEATURE_TILE, last_tile, 0)

    def sent(copy):
        copy.wait_send()

    for c, (row0, size) in enumerate(chunks):
        for distance in range(n_dp - 1):
            forward(row0, size, c, distance, sent)
    for j, peer in enumerate(seq_peers):
        text_copy(seq, peer, j).wait_send()
        stat_copy(seq, peer, j).wait_send()
        weight_copy(seq, peer, j).wait_send()
        relay_copy(peer, j, img).wait_send()


def body_kernel(
    sizes,
    queries,
    out_grad,
    token_image,
    unnormed_keys,
    values,
    key_gain,
    tile_count,
    key_projection_matrix,
    value_projection_matrix,
):
    n_seq, n_dp, heads, group = sizes
    rows, width = unnormed_keys.shape[1:]
    features = key_projection_matrix.shape[0]
    query_rows = n_seq * group * CAP
    chunk_count = rows // CHUNK + 1
    padded = -(-rows // 16) * 16
    vmem = pl.BlockSpec(memory_space=pltpu.VMEM)
    anywhere = pl.BlockSpec(memory_space=pltpu.HBM)
    dma = pltpu.SemaphoreType.DMA
    result = pl.pallas_call(
        functools.partial(kernel, sizes),
        out_shape=pltpu.VMEM((rows, features), jnp.bfloat16),
        in_specs=[
            vmem,
            pl.BlockSpec(memory_space=pltpu.SMEM),
            anywhere,
            anywhere,
            anywhere,
            anywhere,
            vmem,
            anywhere,
            anywhere,
        ],
        out_specs=vmem,
        scratch_shapes=[
            pltpu.VMEM(queries.shape, jnp.bfloat16),
            pltpu.VMEM(queries.shape, jnp.bfloat16),
            pltpu.VMEM((rows, width), jnp.bfloat16),
            pltpu.VMEM((rows, width), jnp.bfloat16),
            pltpu.VMEM((rows, width), jnp.bfloat16),
            pltpu.VMEM((rows % CHUNK, features), jnp.float32),
            pltpu.VMEM((n_seq, 2, heads, group * CAP, HEAD_WIDTH), jnp.bfloat16),
            pltpu.VMEM((heads, rows, query_rows), jnp.float32),
            pltpu.VMEM((heads, rows, query_rows), jnp.float32),
            pltpu.VMEM((n_seq, 8, heads * query_rows), jnp.float32),
            pltpu.VMEM((n_dp, padded, 2 * width), jnp.bfloat16),
            pltpu.VMEM((n_seq, features, 2 * width), jnp.bfloat16),
            dma((4,)),
            dma((n_seq - 1,)),
            dma((n_seq,)),
            dma((n_seq - 1,)),
            dma((n_seq,)),
            dma((2,)),
            dma((n_seq - 1,)),
            dma((n_seq,)),
            dma((n_seq - 1,)),
            dma((n_seq,)),
            dma((2, n_dp - 1, chunk_count)),
            dma((n_dp, chunk_count)),
        ],
        compiler_params=pltpu.CompilerParams(
            collective_id=0, has_side_effects=True, vmem_limit_bytes=VMEM_BYTES - 2 * rows * features
        ),
    )(
        token_image[None],
        tile_count,
        queries,
        out_grad,
        unnormed_keys[0],
        values[0],
        key_gain[None],
        key_projection_matrix,
        value_projection_matrix,
    )
    return result[None]


def body(*args):
    n_seq, n_img, n_dp = (lax.axis_size(name) for name in ("seq", "img", "dp"))
    rows, width = args[3].shape[1:]
    heads = width // HEAD_WIDTH
    group = args[0].shape[1] // width
    fits = n_img == 2 and n_seq == n_dp == 4 and args[7].shape[1] == width and rows % 8 == 0
    if fits and rows % CHUNK and rows % CHUNK % 16 == 8:
        return body_kernel((n_seq, n_dp, heads, group), *args)
    return body_any(*args)


def solution(mesh):
    in_specs = (
        P("seq", "dp"),
        P("seq", "dp"),
        P("seq"),
        P("img", "seq", "dp"),
        P("img", "seq", "dp"),
        P(),
        P(),
        P("dp", "seq"),
        P("dp", "seq"),
    )
    out_specs = P("img", "seq", "dp")
    return jax.shard_map(body, mesh=mesh, in_specs=in_specs, out_specs=out_specs, check_vma=False)
```

profile of v0, /device:TPU:0, one launch (start us, length us, event | category | flops | bytes accessed | tf_op | source)
XLA Modules:
  0.0 137.7 jit_solution(10603180687744253607)
XLA Ops:
  0.0 134.9 %shard_map.91 = bf16[1608,2048]{1,0:T(8,128)(2,1)S(1)} custom-call(s32[1,128]{1,0:T(1,128)} %bitcast.8, s32[2]{0:T(128)} %limit_ref.1, bf16[128,2048]{1,0:T(8,128)(2,1)} %query_hbm.1, bf16[128,2048]{1,0:T(8,128)(2,1)} %grad_hbm.1, bf16[1608,256]{1,0:T(8,128)(2,1)} %bitcast.6, bf16[1608,256]{1,0:T(8,128)(2,1)} %bitcast.7, f32[1,128]{1,0:T(1,128)} %bitcast.9, ...), custom_call_target="tpu_custom_call" | custom-call | tf_op jit(solution)/shard_map/pallas_call | solution.py:530
  134.9 2.8 %copy.11 = bf16[1,1608,2048]{2,1,0:T(8,128)(2,1)} copy(bf16[1,1608,2048]{2,1,0:T(8,128)(2,1)S(1)} %bitcast.5) | data formatting | bytes 13172736
where the time goes:
time: 138 us
  Pallas kernels  135 us (98%)
  local copies, waits for them, and re-layouts  2.8 us (2%)
    pallas_call x1, Pallas kernels, body_kernel(): pl.pallas_call(functools.partial(kernel, sizes), out_shape=pltpu.VMEM((ro...  135 us
    unnamed x1, local copies, waits for them, and re-layouts  2.8 us

commit v1 on v0

v1 whole, which is shorter than its diff:
```python
import functools

import jax
import jax.numpy as jnp
from jax import lax
from jax.experimental import pallas as pl
from jax.experimental.pallas import tpu as pltpu
from jax.sharding import PartitionSpec as P

QUERY_HEAD_COUNT = 64
KEY_VALUE_HEADS = 8
HEAD_WIDTH = 128
TILE_TOK = 1601
TILE_ROWS = 1608
CAP = 16


epsilon = 1e-05
masked = -1e30


def body_any(
    queries,
    out_grad,
    token_image,
    unnormed_keys,
    values,
    key_gain,
    tile_count,
    key_projection_matrix,
    value_projection_matrix,
):
    image_number = lax.axis_index("img")
    seq_index = lax.axis_index("seq")
    attends = token_image == image_number
    slot_rank = jnp.cumsum(attends.astype(jnp.int32)) - 1
    picker = (
        attends[None, :] & (slot_rank[None, :] == jnp.arange(CAP, dtype=jnp.int32)[:, None])
    ).astype(jnp.bfloat16)
    packed_query = jnp.dot(picker, queries, preferred_element_type=jnp.float32).astype(jnp.bfloat16)
    packed_grad = jnp.dot(picker, out_grad, preferred_element_type=jnp.float32).astype(jnp.bfloat16)
    text_query, text_grad = (
        lax.all_gather(packed_query, "seq", axis=0, tiled=True),
        lax.all_gather(packed_grad, "seq", axis=0, tiled=True),
    )
    key_rows = unnormed_keys.shape[1]
    key_width = unnormed_keys.shape[2]
    key_heads = key_width // HEAD_WIDTH
    group_length = QUERY_HEAD_COUNT // KEY_VALUE_HEADS
    text_rows = text_query.shape[0]
    score_scale = HEAD_WIDTH ** (-0.5)
    unnormed_float = unnormed_keys[0].astype(jnp.float32).reshape(key_rows, key_heads, HEAD_WIDTH)
    inverse = lax.rsqrt(jnp.mean(unnormed_float * unnormed_float, axis=-1, keepdims=True) + epsilon)
    unit_key = unnormed_float * inverse
    normed = (unit_key * key_gain).astype(jnp.bfloat16)
    value_heads = values[0].reshape(key_rows, key_heads, HEAD_WIDTH)
    query_heads = text_query.reshape(text_rows, key_heads, group_length, HEAD_WIDTH)
    grad_heads = text_grad.reshape(text_rows, key_heads, group_length, HEAD_WIDTH)
    row_global = seq_index * key_rows + jnp.arange(key_rows, dtype=jnp.int32)
    tile_limit = jnp.sum(
        jnp.where(jnp.arange(tile_count.shape[0], dtype=jnp.int32) == image_number, tile_count, 0)
    )
    live_rows = (row_global // TILE_ROWS < tile_limit) & (row_global % TILE_ROWS < TILE_TOK)
    scores = (
        jnp.einsum("rhge,khe->hgrk", query_heads, normed, preferred_element_type=jnp.float32)
        * score_scale
    )
    scores = jnp.where(live_rows, scores, masked)
    grad_probs = jnp.einsum(
        "rhge,khe->hgrk", grad_heads, value_heads, preferred_element_type=jnp.float32
    )
    row_top = lax.pmax(jnp.max(scores, axis=-1), "seq")
    exponent = jnp.exp(scores - row_top[..., None])
    row_total = lax.psum(jnp.sum(exponent, axis=-1), "seq")
    probabilities = exponent / row_total[..., None]
    inner_sum = lax.psum(jnp.sum(probabilities * grad_probs, axis=-1), "seq")
    probs_low = probabilities.astype(jnp.bfloat16)
    score_grad = (probabilities * (grad_probs - inner_sum[..., None])).astype(jnp.bfloat16)
    value_gradient = jnp.einsum(
        "hgrk,rhge->khe", probs_low, grad_heads, preferred_element_type=jnp.float32
    )
    normalized_gradient = (
        jnp.einsum("hgrk,rhge->khe", score_grad, query_heads, preferred_element_type=jnp.float32)
        * score_scale
    )
    unit_grad = normalized_gradient * key_gain
    key_gradient = inverse * (
        unit_grad - unit_key * jnp.mean(unit_grad * unit_key, axis=-1, keepdims=True)
    )
    key_reduced_precision = key_gradient.astype(jnp.bfloat16).reshape(key_rows, key_width)
    value_reduced_precision = value_gradient.astype(jnp.bfloat16).reshape(key_rows, key_width)
    key_all, value_all = (
        lax.all_gather(key_reduced_precision, "dp", axis=1, tiled=True),
        lax.all_gather(value_reduced_precision, "dp", axis=1, tiled=True),
    )
    contracting = (((1,), (1,)), ((), ()))
    partial_value = lax.dot_general(
        key_all,
        lax.all_gather(key_projection_matrix, "seq", axis=1, tiled=True),
        contracting,
        preferred_element_type=jnp.float32,
    )
    feature_sum = partial_value + lax.dot_general(
        value_all,
        lax.all_gather(value_projection_matrix, "seq", axis=1, tiled=True),
        contracting,
        preferred_element_type=jnp.float32,
    )
    return feature_sum.astype(jnp.bfloat16)[None]


MESH = pl.DeviceIdType.MESH
NT = (((1,), (1,)), ((), ()))
NN = (((1,), (0,)), ((), ()))
CHUNK = 272
FEATURE_TILE = 256
VMEM_BYTES = 67043328


def dot(a, b, dims):
    return lax.dot_general(a, b, dims, preferred_element_type=jnp.float32)


def kernel(
    sizes,
    image_ref,
    limit_ref,
    query_hbm,
    grad_hbm,
    key_hbm,
    value_hbm,
    gain_ref,
    key_weight_ref,
    value_weight_ref,
    out_ref,
    query_ref,
    grad_ref,
    key_ref,
    value_ref,
    normed_ref,
    raw,
    partial,
    text,
    score,
    grad_prob,
    stats,
    outer_stats,
    rows_all,
    weights,
    load_sem,
    text_send,
    text_recv,
    stat_send,
    stat_recv,
    weight_local,
    weight_send,
    weight_recv,
    relay_send,
    relay_recv,
    row_send,
    row_recv,
    raw_send,
    raw_recv,
):
    n_seq, n_dp, heads, group = sizes
    seq = lax.axis_index("seq")
    img = lax.axis_index("img")
    dp = lax.axis_index("dp")
    rows, width = key_ref.shape
    features = key_weight_ref.shape[0]
    half = features // 2
    stack = group * CAP
    query_rows = n_seq * stack
    full = rows // CHUNK
    rest = rows - full * CHUNK
    chunks = [(c * CHUNK, CHUNK) for c in range(full)] + [(full * CHUNK, rest)]
    scale = HEAD_WIDTH ** (-0.5)
    near, far = seq % 2, seq // 2
    seq_peers = [far * 2 + 1 - near, (1 - far) * 2 + near, (1 - far) * 2 + 1 - near]
    step = 1 - 2 * (dp // 2)
    inner, outer, second = dp + step, dp - step, dp + 2 * step
    farthest = (n_dp - 1) * (1 - dp // 2)
    is_end = (dp == 0) | (dp == n_dp - 1)
    is_middle = (dp > 0) & (dp < n_dp - 1)
    extra = heads

    loads = [
        pltpu.make_async_copy(source, target, load_sem.at[k])
        for k, (source, target) in enumerate(
            (
                (query_hbm, query_ref),
                (grad_hbm, grad_ref),
                (key_hbm, key_ref),
                (value_hbm, value_ref),
            )
        )
    ]
    for copy in loads:
        copy.start()

    barrier = pltpu.get_barrier_semaphore()
    for peer in seq_peers:
        pl.semaphore_signal(barrier, inc=1, device_id={"seq": peer}, device_id_type=MESH)
    pl.semaphore_signal(barrier, inc=1, device_id={"img": 1 - img}, device_id_type=MESH)
    pl.semaphore_signal(barrier, inc=1, device_id={"dp": inner}, device_id_type=MESH)

    @pl.when(is_middle)
    def _():
        pl.semaphore_signal(barrier, inc=1, device_id={"dp": outer}, device_id_type=MESH)

    own_weights = [
        pltpu.make_async_copy(
            ref.at[:, pl.ds(h * HEAD_WIDTH, HEAD_WIDTH)],
            weights.at[seq, :, pl.ds((2 * h + k) * HEAD_WIDTH, HEAD_WIDTH)],
            weight_local.at[k, h],
        )
        for k, ref in enumerate((key_weight_ref, value_weight_ref))
        for h in range(heads)
    ]
    for copy in own_weights:
        copy.start()

    tokens = image_ref.shape[1]
    attends = image_ref[...] == img
    upper = (
        lax.broadcasted_iota(jnp.int32, (tokens, tokens), 0)
        <= lax.broadcasted_iota(jnp.int32, (tokens, tokens), 1)
    ).astype(jnp.bfloat16)
    counts = dot(
        jnp.broadcast_to(attends.astype(jnp.float32), (CAP, tokens)).astype(jnp.bfloat16), upper, NN
    )
    slot = lax.broadcasted_iota(jnp.int32, (CAP, tokens), 0).astype(jnp.float32) + 1.0
    picker = jnp.where(attends & (counts == slot), 1.0, 0.0).astype(jnp.bfloat16)

    def raw_copy(k):
        source = (key_hbm, value_hbm)[k]
        return pltpu.make_async_remote_copy(
            src_ref=source.at[:, pl.ds(HEAD_WIDTH, HEAD_WIDTH)],
            dst_ref=raw.at[k],
            send_sem=raw_send.at[k],
            recv_sem=raw_recv.at[k],
            device_id={"dp": outer},
            device_id_type=MESH,
        )

    def text_outer():
        return pltpu.make_async_remote_copy(
            src_ref=text.at[seq, heads - 1],
            dst_ref=text.at[seq, extra],
            send_sem=raw_send.at[2],
            recv_sem=text_recv.at[extra, seq],
            device_id={"dp": outer},
            device_id_type=MESH,
        )

    def stat_outer():
        return pltpu.make_async_remote_copy(
            src_ref=outer_stats.at[0],
            dst_ref=outer_stats.at[1],
            send_sem=raw_send.at[3],
            recv_sem=raw_recv.at[2],
            device_id={"dp": outer},
            device_id_type=MESH,
        )

    def text_copy(h, owner, peer, j):
        return pltpu.make_async_remote_copy(
            src_ref=text.at[owner, h],
            dst_ref=text.at[owner, h],
            send_sem=text_send.at[h, j],
            recv_sem=text_recv.at[h, owner],
            device_id={"seq": peer},
            device_id_type=MESH,
        )

    pl.semaphore_wait(barrier, n_seq - 1 + 1 + 1 + is_middle.astype(jnp.int32))

    @pl.when(is_middle)
    def _():
        raw_copy(0).start()

    for copy in loads[:2]:
        copy.wait()
    for h in range(heads):
        for k, ref in enumerate((query_ref, grad_ref)):
            first = h * group * HEAD_WIDTH
            packed = dot(picker, ref[:, first : first + group * HEAD_WIDTH], NN).astype(jnp.bfloat16)
            for g in range(group):
                column = g * HEAD_WIDTH
                text[seq, h, k, g * CAP : (g + 1) * CAP, :] = packed[:, column : column + HEAD_WIDTH]
        for j, peer in enumerate(seq_peers):
            text_copy(h, seq, peer, j).start()

    @pl.when(is_middle)
    def _():
        text_outer().start()
        raw_copy(1).start()

    gain = gain_ref[...]
    live_limit = limit_ref[img]

    def unit_of(k):
        inverse = lax.rsqrt(jnp.mean(k * k, axis=-1, keepdims=True) + epsilon)
        return k * inverse, inverse

    def own_key(row0, size, h):
        return key_ref[pl.ds(row0, size), h * HEAD_WIDTH : (h + 1) * HEAD_WIDTH].astype(jnp.float32)

    def text_of(h, k):
        return text[:, h, k].reshape(query_rows, HEAD_WIDTH)

    def live_of(row0, size):
        row = seq * rows + row0 + lax.broadcasted_iota(jnp.int32, (size, 1), 0)
        return (row // TILE_ROWS < live_limit) & (row % TILE_ROWS < TILE_TOK)

    def over_chunks(act, carry):
        carry = lax.fori_loop(
            0, full, lambda i, c: act(pl.multiple_of(i * CHUNK, 16), CHUNK, c), carry
        )
        return act(full * CHUNK, rest, carry)

    for copy in loads[2:]:
        copy.wait()

    def normalize_chunk(row0, size, carry):
        for h in range(heads):
            unit, _ = unit_of(own_key(row0, size, h))
            normed_ref[pl.ds(row0, size), h * HEAD_WIDTH : (h + 1) * HEAD_WIDTH] = (
                unit * gain
            ).astype(jnp.bfloat16)
        return carry

    over_chunks(normalize_chunk, 0)

    def stat_copy(h, owner, peer, j):
        return pltpu.make_async_remote_copy(
            src_ref=stats.at[owner, h],
            dst_ref=stats.at[owner, h],
            send_sem=stat_send.at[h, j],
            recv_sem=stat_recv.at[h, owner],
            device_id={"seq": peer},
            device_id_type=MESH,
        )

    for h in range(heads):
        lanes = slice(h * HEAD_WIDTH, (h + 1) * HEAD_WIDTH)
        for j, owner in enumerate(seq_peers):
            text_copy(h, owner, owner, j).wait_recv()

        def first_pass(row0, size, top):
            s = dot(normed_ref[pl.ds(row0, size), lanes], text_of(h, 0), NT) * scale
            s = jnp.where(live_of(row0, size), s, masked)
            score[h, pl.ds(row0, size), :] = s
            return jnp.maximum(top, jnp.max(s, axis=0, keepdims=True))

        top = over_chunks(first_pass, jnp.full((1, query_rows), masked, jnp.float32))

        def second_pass(row0, size, sums):
            e = jnp.exp(score[h, pl.ds(row0, size), :] - top)
            p = dot(value_ref[pl.ds(row0, size), lanes], text_of(h, 1), NT)
            score[h, pl.ds(row0, size), :] = e
            grad_prob[h, pl.ds(row0, size), :] = p
            return (
                sums[0] + jnp.sum(e, axis=0, keepdims=True),
                sums[1] + jnp.sum(e * p, axis=0, keepdims=True),
            )

        sums = over_chunks(
            second_pass, tuple(jnp.zeros((1, query_rows), jnp.float32) for _ in range(2))
        )
        stats[seq, h, 0:1, :] = top
        stats[seq, h, 1:2, :] = sums[0]
        stats[seq, h, 2:3, :] = sums[1]
        stats[seq, h, 3:8, :] = jnp.zeros((5, query_rows), jnp.float32)
        for j, peer in enumerate(seq_peers):
            stat_copy(h, seq, peer, j).start()

    @pl.when(is_end)
    def _():
        text_outer().wait_recv()
        for j, peer in enumerate(seq_peers):
            text_copy(extra, seq, peer, j).start()

    def weight_copy(owner, peer, j):
        part = weights.at[owner, pl.ds(pl.multiple_of(img * half, half), half)]
        return pltpu.make_async_remote_copy(
            src_ref=part,
            dst_ref=part,
            send_sem=weight_send.at[j],
            recv_sem=weight_recv.at[owner],
            device_id={"seq": peer},
            device_id_type=MESH,
        )

    def relay_copy(owner, j, which):
        part = weights.at[owner, pl.ds(pl.multiple_of(which * half, half), half)]
        return pltpu.make_async_remote_copy(
            src_ref=part,
            dst_ref=part,
            send_sem=relay_send.at[j],
            recv_sem=relay_recv.at[owner],
            device_id={"img": 1 - img},
            device_id_type=MESH,
        )

    for copy in own_weights:
        copy.wait()
    for j, peer in enumerate(seq_peers):
        weight_copy(seq, peer, j).start()

    def combine(h):
        for j, peer in enumerate(seq_peers):
            stat_copy(h, peer, peer, j).wait_recv()
        tops = [stats[i, h, 0:1, :] for i in range(n_seq)]
        top = functools.reduce(jnp.maximum, tops)
        factors = [jnp.exp(t - top) for t in tops]
        total = sum(f * stats[i, h, 1:2, :] for i, f in enumerate(factors))
        inner_sum = sum(f * stats[i, h, 2:3, :] for i, f in enumerate(factors)) / total
        own = jnp.exp(stats[seq, h, 0:1, :] - top) / total
        return top, 1.0 / total, inner_sum, own

    def row_copy(kind, owner, h, c, row0, size, peer):
        lane0, lanes = (0, 2 * width) if h is None else (2 * h * HEAD_WIDTH, 2 * HEAD_WIDTH)
        part = rows_all.at[owner, pl.ds(row0, size), pl.ds(lane0, lanes)]
        return pltpu.make_async_remote_copy(
            src_ref=part,
            dst_ref=part,
            send_sem=row_send.at[kind, c],
            recv_sem=row_recv.at[owner, 0 if h == 0 else 1, c],
            device_id={"dp": peer},
            device_id_type=MESH,
        )

    def arrive(owner, h, c, row0, size):
        row_copy(0, owner, h, c, row0, size, inner).wait_recv()

    def own_inner(h, c, row0, size):
        return row_copy(h, dp, h, c, row0, size, inner)

    def own_outer(c, row0, size):
        return row_copy(2, dp, 0, c, row0, size, outer)

    def inner_outer(h, c, row0, size):
        return row_copy(3 + h, inner, h, c, row0, size, outer)

    def far_outer(c, row0, size):
        return row_copy(5, farthest, None, c, row0, size, outer)

    def outer_inner(c, row0, size):
        return row_copy(6, outer, None, c, row0, size, inner)

    def finish(owner, h, which, row0, size, p, g, unit, inverse):
        value_gradient = dot(p.astype(jnp.bfloat16), text_of(which, 1), NN)
        unit_grad = dot(g.astype(jnp.bfloat16), text_of(which, 0), NN) * scale * gain
        key_gradient = inverse * (
            unit_grad - unit * jnp.mean(unit_grad * unit, axis=-1, keepdims=True)
        )
        lane = 2 * h * HEAD_WIDTH
        rows_all[owner, pl.ds(row0, size), lane : lane + HEAD_WIDTH] = key_gradient.astype(
            jnp.bfloat16
        )
        lane = lane + HEAD_WIDTH
        rows_all[owner, pl.ds(row0, size), lane : lane + HEAD_WIDTH] = value_gradient.astype(
            jnp.bfloat16
        )

    for h in range(heads):
        top, inverse_total, inner_sum, own_factor = combine(h)
        if h == heads - 1:
            outer_stats[0, 0:1, :] = top
            outer_stats[0, 1:2, :] = inverse_total
            outer_stats[0, 2:3, :] = inner_sum
            outer_stats[0, 3:8, :] = jnp.zeros((5, query_rows), jnp.float32)

            @pl.when(is_middle)
            def _():
                stat_outer().start()

        def own_pass(c, row0, size):
            p = score[h, pl.ds(row0, size), :] * own_factor
            g = p * (grad_prob[h, pl.ds(row0, size), :] - inner_sum)
            finish(dp, h, h, row0, size, p, g, *unit_of(own_key(row0, size, h)))
            own_inner(h, c, row0, size).start()
            if h == 0:

                @pl.when(is_middle)
                def _():
                    own_outer(c, row0, size).start()

        def own_chunk(i, _):
            own_pass(i, pl.multiple_of(i * CHUNK, 16), CHUNK)
            return 0

        lax.fori_loop(0, full, own_chunk, 0)
        own_pass(full, full * CHUNK, rest)

    @pl.when(is_middle)
    def _():
        for c, (row0, size) in enumerate(chunks):
            arrive(outer, 0, c, row0, size)
            arrive(inner, 0, c, row0, size)
            inner_outer(0, c, row0, size).start()
        for c, (row0, size) in enumerate(chunks):
            arrive(inner, 1, c, row0, size)
            inner_outer(1, c, row0, size).start()
            arrive(outer, 1, c, row0, size)
            outer_inner(c, row0, size).start()

    @pl.when(is_end)
    def _():
        for j, owner in enumerate(seq_peers):
            text_copy(extra, owner, owner, j).wait_recv()
        for k in range(2):
            raw_copy(k).wait_recv()
        stat_outer().wait_recv()
        top = outer_stats[1, 0:1, :]
        inverse_total = outer_stats[1, 1:2, :]
        inner_sum = outer_stats[1, 2:3, :]

        def extra_pass(row0, size, carry):
            unit, inverse = unit_of(raw[0, pl.ds(row0, size), :].astype(jnp.float32))
            s = dot((unit * gain).astype(jnp.bfloat16), text_of(extra, 0), NT) * scale
            s = jnp.where(live_of(row0, size), s, masked)
            p = jnp.exp(s - top) * inverse_total
            g = p * (dot(raw[1, pl.ds(row0, size), :], text_of(extra, 1), NT) - inner_sum)
            finish(inner, heads - 1, extra, row0, size, p, g, unit, inverse)
            return carry

        over_chunks(extra_pass, 0)

    for j, peer in enumerate(seq_peers):
        weight_copy(peer, peer, j).wait_recv()
        relay_copy(peer, j, img).start()

    @pl.when(is_end)
    def _():
        for c, (row0, size) in enumerate(chunks):
            arrive(inner, 0, c, row0, size)
        for h in range(heads):
            for c, (row0, size) in enumerate(chunks):
                arrive(second, h, c, row0, size)

    for j, peer in enumerate(seq_peers):
        relay_copy(peer, j, 1 - img).wait_recv()

    def last_product(block, column):
        return dot(
            rows_all[block, full * CHUNK : rows, :],
            weights[block, pl.ds(column, FEATURE_TILE), :],
            NT,
        )

    def partial_tile(i, _):
        column = pl.multiple_of(i * FEATURE_TILE, FEATURE_TILE)
        partial[:, pl.ds(column, FEATURE_TILE)] = functools.reduce(
            jnp.add, [last_product(dp // 2 + b, column) for b in range(n_dp - 1)]
        )
        return 0

    def last_tile(i, _):
        column = pl.multiple_of(i * FEATURE_TILE, FEATURE_TILE)
        total = partial[:, pl.ds(column, FEATURE_TILE)] + last_product(farthest, column)
        out_ref[full * CHUNK : rows, pl.ds(column, FEATURE_TILE)] = total.astype(out_ref.dtype)
        return 0

    def multiply(row0, size):
        def tile(i, _):
            column = pl.multiple_of(i * FEATURE_TILE, FEATURE_TILE)
            total = functools.reduce(
                jnp.add,
                [
                    dot(
                        rows_all[b, pl.ds(row0, size), :],
                        weights[b, pl.ds(column, FEATURE_TILE), :],
                        NT,
                    )
                    for b in range(n_dp)
                ],
            )
            out_ref[pl.ds(row0, size), pl.ds(column, FEATURE_TILE)] = total.astype(out_ref.dtype)
            return 0

        lax.fori_loop(0, features // FEATURE_TILE, tile, 0)

    def last_arrival(c, row0, size):
        arrive(farthest, None, c, row0, size)

        @pl.when(is_middle)
        def _():
            far_outer(c, row0, size).start()

    def finish_chunk(i, _):
        row0 = pl.multiple_of(i * CHUNK, 16)
        last_arrival(i, row0, CHUNK)
        multiply(row0, CHUNK)
        return 0

    lax.fori_loop(0, features // FEATURE_TILE, partial_tile, 0)
    lax.fori_loop(0, full, finish_chunk, 0)
    last_arrival(full, full * CHUNK, rest)
    lax.fori_loop(0, features // FEATURE_TILE, last_tile, 0)

    for c, (row0, size) in enumerate(chunks):
        for h in range(heads):
            own_inner(h, c, row0, size).wait_send()

    @pl.when(is_middle)
    def _():
        for k in range(2):
            raw_copy(k).wait_send()
        text_outer().wait_send()
        stat_outer().wait_send()
        for c, (row0, size) in enumerate(chunks):
            own_outer(c, row0, size).wait_send()
            for h in range(heads):
                inner_outer(h, c, row0, size).wait_send()
            outer_inner(c, row0, size).wait_send()
            far_outer(c, row0, size).wait_send()

    @pl.when(is_end)
    def _():
        for j, peer in enumerate(seq_peers):
            text_copy(extra, seq, peer, j).wait_send()

    for j, peer in enumerate(seq_peers):
        for h in range(heads):
            text_copy(h, seq, peer, j).wait_send()
            stat_copy(h, seq, peer, j).wait_send()
        weight_copy(seq, peer, j).wait_send()
        relay_copy(peer, j, img).wait_send()


def body_kernel(
    sizes,
    queries,
    out_grad,
    token_image,
    unnormed_keys,
    values,
    key_gain,
    tile_count,
    key_projection_matrix,
    value_projection_matrix,
):
    n_seq, n_dp, heads, group = sizes
    rows, width = unnormed_keys.shape[1:]
    features = key_projection_matrix.shape[0]
    query_rows = n_seq * group * CAP
    chunk_count = rows // CHUNK + 1
    padded = -(-rows // 16) * 16
    vmem = pl.BlockSpec(memory_space=pltpu.VMEM)
    anywhere = pl.BlockSpec(memory_space=pltpu.HBM)
    dma = pltpu.SemaphoreType.DMA
    result = pl.pallas_call(
        functools.partial(kernel, sizes),
        out_shape=pltpu.VMEM((rows, features), jnp.bfloat16),
        in_specs=[
            vmem,
            pl.BlockSpec(memory_space=pltpu.SMEM),
            anywhere,
            anywhere,
            anywhere,
            anywhere,
            vmem,
            anywhere,
            anywhere,
        ],
        out_specs=vmem,
        scratch_shapes=[
            pltpu.VMEM(queries.shape, jnp.bfloat16),
            pltpu.VMEM(queries.shape, jnp.bfloat16),
            pltpu.VMEM((rows, width), jnp.bfloat16),
            pltpu.VMEM((rows, width), jnp.bfloat16),
            pltpu.VMEM((rows, width), jnp.bfloat16),
            pltpu.VMEM((2, rows, HEAD_WIDTH), jnp.bfloat16),
            pltpu.VMEM((rows % CHUNK, features), jnp.float32),
            pltpu.VMEM((n_seq, heads + 1, 2, group * CAP, HEAD_WIDTH), jnp.bfloat16),
            pltpu.VMEM((heads, rows, query_rows), jnp.float32),
            pltpu.VMEM((heads, rows, query_rows), jnp.float32),
            pltpu.VMEM((n_seq, heads, 8, query_rows), jnp.float32),
            pltpu.VMEM((2, 8, query_rows), jnp.float32),
            pltpu.VMEM((n_dp, padded, 2 * width), jnp.bfloat16),
            pltpu.VMEM((n_seq, features, 2 * width), jnp.bfloat16),
            dma((4,)),
            dma((heads + 1, n_seq - 1)),
            dma((heads + 1, n_seq)),
            dma((heads, n_seq - 1)),
            dma((heads, n_seq)),
            dma((2, heads)),
            dma((n_seq - 1,)),
            dma((n_seq,)),
            dma((n_seq - 1,)),
            dma((n_seq,)),
            dma((7, chunk_count)),
            dma((n_dp, 2, chunk_count)),
            dma((4,)),
            dma((3,)),
        ],
        compiler_params=pltpu.CompilerParams(
            collective_id=0, has_side_effects=True, vmem_limit_bytes=VMEM_BYTES - 2 * rows * features
        ),
    )(
        token_image[None],
        tile_count,
        queries,
        out_grad,
        unnormed_keys[0],
        values[0],
        key_gain[None],
        key_projection_matrix,
        value_projection_matrix,
    )
    return result[None]


def body(*args):
    n_seq, n_img, n_dp = (lax.axis_size(name) for name in ("seq", "img", "dp"))
    rows, width = args[3].shape[1:]
    heads = width // HEAD_WIDTH
    group = args[0].shape[1] // width
    fits = n_img == heads == 2 and n_seq == n_dp == 4 and args[7].shape[1] == width and rows % 8 == 0
    if fits and rows % CHUNK and rows % CHUNK % 16 == 8:
        return body_kernel((n_seq, n_dp, heads, group), *args)
    return body_any(*args)


def solution(mesh):
    in_specs = (
        P("seq", "dp"),
        P("seq", "dp"),
        P("seq"),
        P("img", "seq", "dp"),
        P("img", "seq", "dp"),
        P(),
        P(),
        P("dp", "seq"),
        P("dp", "seq"),
    )
    out_specs = P("img", "seq", "dp")
    return jax.shard_map(body, mesh=mesh, in_specs=in_specs, out_specs=out_specs, check_vma=False)
```

time: 138 us -> 121 us (0.88)
  Pallas kernels: 135 us -> 118 us
    pallas_call x1, Pallas kernels: 135 us -> 118 us  [body_kernel(): pl.pallas_call(functools.partial(kernel, sizes), out_shape=pltpu.VMEM((ro...]
where the time goes in v1:
time: 121 us
  Pallas kernels  118 us (98%)
  local copies, waits for them, and re-layouts  2.8 us (2%)
    pallas_call x1, Pallas kernels, body_kernel(): pl.pallas_call(functools.partial(kernel, sizes), out_shape=pltpu.VMEM((ro...  118 us
    unnamed x1, local copies, waits for them, and re-layouts  2.8 us

profile of v1, /device:TPU:0, one launch (start us, length us, event | category | flops | bytes accessed | tf_op | source)
XLA Modules:
  0.0 120.9 jit_solution(10128299465764835244)
XLA Ops:
  0.0 118.1 %shard_map.91 = bf16[1608,2048]{1,0:T(8,128)(2,1)S(1)} custom-call(s32[1,128]{1,0:T(1,128)} %bitcast.8, s32[2]{0:T(128)} %limit_ref.1, bf16[128,2048]{1,0:T(8,128)(2,1)} %query_hbm.1, bf16[128,2048]{1,0:T(8,128)(2,1)} %grad_hbm.1, bf16[1608,256]{1,0:T(8,128)(2,1)} %bitcast.6, bf16[1608,256]{1,0:T(8,128)(2,1)} %bitcast.7, f32[1,128]{1,0:T(1,128)} %bitcast.9, ...), custom_call_target="tpu_custom_call" | custom-call | tf_op jit(solution)/shard_map/pallas_call | solution.py:654
  118.1 2.8 %copy.11 = bf16[1,1608,2048]{2,1,0:T(8,128)(2,1)} copy(bf16[1,1608,2048]{2,1,0:T(8,128)(2,1)S(1)} %bitcast.5) | data formatting | bytes 13172736

commit v2 on v1

--- a/solution.py
+++ b/solution.py
@@ -208,30 +208,6 @@
     def _():
         pl.semaphore_signal(barrier, inc=1, device_id={"dp": outer}, device_id_type=MESH)
 
-    own_weights = [
-        pltpu.make_async_copy(
-            ref.at[:, pl.ds(h * HEAD_WIDTH, HEAD_WIDTH)],
-            weights.at[seq, :, pl.ds((2 * h + k) * HEAD_WIDTH, HEAD_WIDTH)],
-            weight_local.at[k, h],
-        )
-        for k, ref in enumerate((key_weight_ref, value_weight_ref))
-        for h in range(heads)
-    ]
-    for copy in own_weights:
-        copy.start()
-
-    tokens = image_ref.shape[1]
-    attends = image_ref[...] == img
-    upper = (
-        lax.broadcasted_iota(jnp.int32, (tokens, tokens), 0)
-        <= lax.broadcasted_iota(jnp.int32, (tokens, tokens), 1)
-    ).astype(jnp.bfloat16)
-    counts = dot(
-        jnp.broadcast_to(attends.astype(jnp.float32), (CAP, tokens)).astype(jnp.bfloat16), upper, NN
-    )
-    slot = lax.broadcasted_iota(jnp.int32, (CAP, tokens), 0).astype(jnp.float32) + 1.0
-    picker = jnp.where(attends & (counts == slot), 1.0, 0.0).astype(jnp.bfloat16)
-
     def raw_copy(k):
         source = (key_hbm, value_hbm)[k]
         return pltpu.make_async_remote_copy(
@@ -243,6 +219,36 @@
             device_id_type=MESH,
         )
 
+    pl.semaphore_wait(barrier, n_seq - 1 + 1 + 1 + is_middle.astype(jnp.int32))
+
+    @pl.when(is_middle)
+    def _():
+        raw_copy(0).start()
+
+    own_weights = [
+        pltpu.make_async_copy(
+            ref.at[:, pl.ds(h * HEAD_WIDTH, HEAD_WIDTH)],
+            weights.at[seq, :, pl.ds((2 * h + k) * HEAD_WIDTH, HEAD_WIDTH)],
+            weight_local.at[k, h],
+        )
+        for k, ref in enumerate((key_weight_ref, value_weight_ref))
+        for h in range(heads)
+    ]
+    for copy in own_weights:
+        copy.start()
+
+    tokens = image_ref.shape[1]
+    attends = image_ref[...] == img
+    upper = (
+        lax.broadcasted_iota(jnp.int32, (tokens, tokens), 0)
+        <= lax.broadcasted_iota(jnp.int32, (tokens, tokens), 1)
+    ).astype(jnp.bfloat16)
+    counts = dot(
+        jnp.broadcast_to(attends.astype(jnp.float32), (CAP, tokens)).astype(jnp.bfloat16), upper, NN
+    )
+    slot = lax.broadcasted_iota(jnp.int32, (CAP, tokens), 0).astype(jnp.float32) + 1.0
+    picker = jnp.where(attends & (counts == slot), 1.0, 0.0).astype(jnp.bfloat16)
+
     def text_outer():
         return pltpu.make_async_remote_copy(
             src_ref=text.at[seq, heads - 1],
@@ -272,12 +278,6 @@
             device_id={"seq": peer},
             device_id_type=MESH,
         )
-
-    pl.semaphore_wait(barrier, n_seq - 1 + 1 + 1 + is_middle.astype(jnp.int32))
-
-    @pl.when(is_middle)
-    def _():
-        raw_copy(0).start()
 
     for copy in loads[:2]:
         copy.wait()
@@ -598,7 +598,7 @@
     lax.fori_loop(0, features // FEATURE_TILE, partial_tile, 0)
     lax.fori_loop(0, full, finish_chunk, 0)
     last_arrival(full, full * CHUNK, rest)
-    lax.fori_loop(0, features // FEATURE_TILE, last_tile, 0)
+    lax.fori_loop(0, features // FEATURE_TILE, last_tile, 0, unroll=True)
 
     for c, (row0, size) in enumerate(chunks):
         for h in range(heads):

time: 121 us -> 120 us (level)
    pallas_call x1, Pallas kernels: 118 us -> 117 us  [body_kernel(): pl.pallas_call(functools.partial(kernel, sizes), out_shape=pltpu.VMEM((ro...]
where the time goes in v2:
time: 120 us
  Pallas kernels  117 us (98%)
  local copies, waits for them, and re-layouts  2.8 us (2%)
    pallas_call x1, Pallas kernels, body_kernel(): pl.pallas_call(functools.partial(kernel, sizes), out_shape=pltpu.VMEM((ro...  117 us
    unnamed x1, local copies, waits for them, and re-layouts  2.8 us

profile of v2, /device:TPU:0, one launch (start us, length us, event | category | flops | bytes accessed | tf_op | source)
XLA Modules:
  0.0 119.6 jit_solution(7267271336069928255)
XLA Ops:
  0.0 116.8 %shard_map.91 = bf16[1608,2048]{1,0:T(8,128)(2,1)S(1)} custom-call(s32[1,128]{1,0:T(1,128)} %bitcast.8, s32[2]{0:T(128)} %limit_ref.1, bf16[128,2048]{1,0:T(8,128)(2,1)} %query_hbm.1, bf16[128,2048]{1,0:T(8,128)(2,1)} %grad_hbm.1, bf16[1608,256]{1,0:T(8,128)(2,1)} %bitcast.6, bf16[1608,256]{1,0:T(8,128)(2,1)} %bitcast.7, f32[1,128]{1,0:T(1,128)} %bitcast.9, ...), custom_call_target="tpu_custom_call" | custom-call | tf_op jit(solution)/shard_map/pallas_call | solution.py:654
  116.8 2.8 %copy.11 = bf16[1,1608,2048]{2,1,0:T(8,128)(2,1)} copy(bf16[1,1608,2048]{2,1,0:T(8,128)(2,1)S(1)} %bitcast.5) | data formatting | bytes 13172736

commit v3 on v2

--- a/solution.py
+++ b/solution.py
@@ -161,6 +161,7 @@
     row_recv,
     raw_send,
     raw_recv,
+    entered,
 ):
     n_seq, n_dp, heads, group = sizes
     seq = lax.axis_index("seq")
@@ -199,7 +200,7 @@
         copy.start()
 
     barrier = pltpu.get_barrier_semaphore()
-    for peer in seq_peers:
+    for peer in seq_peers[:2]:
         pl.semaphore_signal(barrier, inc=1, device_id={"seq": peer}, device_id_type=MESH)
     pl.semaphore_signal(barrier, inc=1, device_id={"img": 1 - img}, device_id_type=MESH)
     pl.semaphore_signal(barrier, inc=1, device_id={"dp": inner}, device_id_type=MESH)
@@ -219,11 +220,13 @@
             device_id_type=MESH,
         )
 
-    pl.semaphore_wait(barrier, n_seq - 1 + 1 + 1 + is_middle.astype(jnp.int32))
+    pl.semaphore_wait(barrier, 2 + 1 + 1 + is_middle.astype(jnp.int32))
 
     @pl.when(is_middle)
     def _():
         raw_copy(0).start()
+
+    pl.semaphore_signal(entered, inc=1, device_id={"seq": seq_peers[0]}, device_id_type=MESH)
 
     own_weights = [
         pltpu.make_async_copy(
@@ -289,6 +292,8 @@
                 column = g * HEAD_WIDTH
                 text[seq, h, k, g * CAP : (g + 1) * CAP, :] = packed[:, column : column + HEAD_WIDTH]
         for j, peer in enumerate(seq_peers):
+            if h == 0 and j == 2:
+                pl.semaphore_wait(entered, 1)
             text_copy(h, seq, peer, j).start()
 
     @pl.when(is_middle)
@@ -417,7 +422,7 @@
         total = sum(f * stats[i, h, 1:2, :] for i, f in enumerate(factors))
         inner_sum = sum(f * stats[i, h, 2:3, :] for i, f in enumerate(factors)) / total
         own = jnp.exp(stats[seq, h, 0:1, :] - top) / total
-        return top, 1.0 / total, inner_sum, own
+        return top + jnp.log(total), inner_sum, own
 
     def row_copy(kind, owner, h, c, row0, size, peer):
         lane0, lanes = (0, 2 * width) if h is None else (2 * h * HEAD_WIDTH, 2 * HEAD_WIDTH)
@@ -465,12 +470,12 @@
         )
 
     for h in range(heads):
-        top, inverse_total, inner_sum, own_factor = combine(h)
+        log_total, inner_sum, own_factor = combine(h)
         if h == heads - 1:
-            outer_stats[0, 0:1, :] = top
-            outer_stats[0, 1:2, :] = inverse_total
-            outer_stats[0, 2:3, :] = inner_sum
-            outer_stats[0, 3:8, :] = jnp.zeros((5, query_rows), jnp.float32)
+            for i in range(n_seq):
+                part = slice(i * stack, (i + 1) * stack)
+                outer_stats[0, i : i + 1, :] = log_total[:, part]
+                outer_stats[0, n_seq + i : n_seq + i + 1, :] = inner_sum[:, part]
 
             @pl.when(is_middle)
             def _():
@@ -513,15 +518,16 @@
         for k in range(2):
             raw_copy(k).wait_recv()
         stat_outer().wait_recv()
-        top = outer_stats[1, 0:1, :]
-        inverse_total = outer_stats[1, 1:2, :]
-        inner_sum = outer_stats[1, 2:3, :]
+        log_total, inner_sum = (
+            jnp.concatenate([outer_stats[1, i + j : i + j + 1, :] for j in range(n_seq)], axis=1)
+            for i in (0, n_seq)
+        )
 
         def extra_pass(row0, size, carry):
             unit, inverse = unit_of(raw[0, pl.ds(row0, size), :].astype(jnp.float32))
             s = dot((unit * gain).astype(jnp.bfloat16), text_of(extra, 0), NT) * scale
             s = jnp.where(live_of(row0, size), s, masked)
-            p = jnp.exp(s - top) * inverse_total
+            p = jnp.exp(s - log_total)
             g = p * (dot(raw[1, pl.ds(row0, size), :], text_of(extra, 1), NT) - inner_sum)
             finish(inner, heads - 1, extra, row0, size, p, g, unit, inverse)
             return carry
@@ -678,7 +684,7 @@
             pltpu.VMEM((heads, rows, query_rows), jnp.float32),
             pltpu.VMEM((heads, rows, query_rows), jnp.float32),
             pltpu.VMEM((n_seq, heads, 8, query_rows), jnp.float32),
-            pltpu.VMEM((2, 8, query_rows), jnp.float32),
+            pltpu.VMEM((2, 2 * n_seq, group * CAP), jnp.float32),
             pltpu.VMEM((n_dp, padded, 2 * width), jnp.bfloat16),
             pltpu.VMEM((n_seq, features, 2 * width), jnp.bfloat16),
             dma((4,)),
@@ -695,6 +701,7 @@
             dma((n_dp, 2, chunk_count)),
             dma((4,)),
             dma((3,)),
+            pltpu.SemaphoreType.REGULAR,
         ],
         compiler_params=pltpu.CompilerParams(
             collective_id=0, has_side_effects=True, vmem_limit_bytes=VMEM_BYTES - 2 * rows * features

time: 120 us -> 119 us (level)
  no operation moved by 1% of the time
where the time goes in v3:
time: 119 us; the launch traced here: 118 us
  Pallas kernels  116 us (97%)
  local copies, waits for them, and re-layouts  2.8 us (2%)
    pallas_call x1, Pallas kernels, body_kernel(): pl.pallas_call(functools.partial(kernel, sizes), out_shape=pltpu.VMEM((ro...  116 us
    unnamed x1, local copies, waits for them, and re-layouts  2.8 us

profile of v3, /device:TPU:0, one launch (start us, length us, event | category | flops | bytes accessed | tf_op | source)
XLA Modules:
  0.0 118.5 jit_solution(10147201158009538364)
XLA Ops:
  0.0 115.7 %shard_map.91 = bf16[1608,2048]{1,0:T(8,128)(2,1)S(1)} custom-call(s32[1,128]{1,0:T(1,128)} %bitcast.8, s32[2]{0:T(128)} %limit_ref.1, bf16[128,2048]{1,0:T(8,128)(2,1)} %query_hbm.1, bf16[128,2048]{1,0:T(8,128)(2,1)} %grad_hbm.1, bf16[1608,256]{1,0:T(8,128)(2,1)} %bitcast.6, bf16[1608,256]{1,0:T(8,128)(2,1)} %bitcast.7, f32[1,128]{1,0:T(1,128)} %bitcast.9, ...), custom_call_target="tpu_custom_call" | custom-call | tf_op jit(solution)/shard_map/pallas_call | solution.py:660
  115.7 2.8 %copy.11 = bf16[1,1608,2048]{2,1,0:T(8,128)(2,1)} copy(bf16[1,1608,2048]{2,1,0:T(8,128)(2,1)S(1)} %bitcast.5) | data formatting | bytes 13172736
